TPU v7x, 32 devices: a whole 2x2x4 slice. The times are simulated.
32 devices in a mesh: groups: 2 (over x), tensor: 16 (over z, y, core).
Axes of the slice: x: 2, y: 2, z: 4, core: 2. Of those that a mesh axis runs over, the one named last changes fastest.
Arguments:
- tokens: bfloat16 [64, 8192], P(('groups', 'tensor')), parts along dimension 0, may hold values from -6 to 6
- cotangent: bfloat16 [64, 8192], P(('groups', 'tensor')), parts along dimension 0, may hold values from -6 to 6
- up_blocks: bfloat16 [512, 128, 128], P('tensor'), may hold values from -0.1875 to 0.1875
- gate_blocks: bfloat16 [512, 128, 128], P('tensor'), may hold values from -0.1875 to 0.1875
- down_blocks: bfloat16 [512, 128, 128], P('tensor'), may hold values from -0.21875 to 0.21875
- up_layout: int32 [512], P('tensor'), may hold values from 0 to 191, as said below
- gate_layout: int32 [512], P('tensor'), may hold values from 0 to 191, as said below
- down_layout: int32 [512], P('tensor'), may hold values from 0 to 191, as said below
- live_counts: int32 [3, 16], P(None, 'tensor'), may hold values from 4 to 32, as said below
Outputs:
- output: bfloat16 [64, 8192], P(('groups', 'tensor')), parts along dimension 0
- grad_tokens: bfloat16 [64, 8192], P(('groups', 'tensor')), parts along dimension 0
- grad_up: bfloat16 [1024, 128, 128], P(('groups', 'tensor')), parts along dimension 0
- grad_gate: bfloat16 [1024, 128, 128], P(('groups', 'tensor')), parts along dimension 0
- grad_down: bfloat16 [1024, 128, 128], P(('groups', 'tensor')), parts along dimension 0
There are 2 independent parts, one for each index of `groups`. A program takes and returns all parts, laid end to end along the dimension named above; an argument that names none is the same for every part. Nothing has to cross between parts.
Inputs may be any that keep to these rules, and one draw needn't show every extreme that they name: `up_layout`: within the 32 slots of one owner the codes of one matrix are all different. `gate_layout`: within the 32 slots of one owner the codes of one matrix are all different. `down_layout`: within the 32 slots of one owner the codes of one matrix are all different. `live_counts`: in each of the three rows some owner has exactly 32 live slots; slots past an owner's count hold blocks that are not used.
All inputs are finite; a program needn't handle non-finite values.
Results may differ from a plain program's by a relative error of at most 0.0051.
Values may be sent and summed in bfloat16 or wider, within the bound.
A program may use at most 64 MiB of HBM per device.

v0:
```python
import jax
import jax.numpy as jnp
from jax import lax
from jax.sharding import PartitionSpec as P

HB_DEV = 3


def slot_tables(layout, count, major_size):
    slot_total = layout.shape[0]
    major = layout // HB_DEV
    minor = layout % HB_DEV
    live_mask = (jnp.arange(slot_total) < count).astype(jnp.float32)
    major_hot = (major[:, None] == jnp.arange(major_size)[None, :]).astype(jnp.float32)
    minor_hot = (minor[:, None] == jnp.arange(HB_DEV)[None, :]).astype(jnp.float32)
    return (major, minor, live_mask, major_hot, minor_hot)


def local(
    tokens,
    cotangent,
    up_blocks,
    gate_blocks,
    down_blocks,
    up_layout,
    gate_layout,
    down_layout,
    live_counts,
):
    highest = lax.Precision.HIGHEST
    f32 = jnp.float32
    x_full = lax.all_gather(tokens, "tensor", axis=0, tiled=True)
    dy_full = lax.all_gather(cotangent, "tensor", axis=0, tiled=True)
    row_total = x_full.shape[0]
    block_size = up_blocks.shape[1]
    width_blocks = x_full.shape[1] // block_size
    x_split = x_full.reshape(row_total, width_blocks, block_size)
    count_trio = live_counts[:, 0]
    up_major, up_minor, up_live, up_rowhot, up_hidhot = slot_tables(
        up_layout, count_trio[0], width_blocks
    )
    gate_major, gate_minor, gate_live, gate_rowhot, gate_hidhot = slot_tables(
        gate_layout, count_trio[1], width_blocks
    )
    down_major, down_minor, down_live, down_colhot, down_hidhot = slot_tables(
        down_layout, count_trio[2], width_blocks
    )
    w_up = up_blocks * up_live[:, None, None].astype(jnp.bfloat16)
    w_gate = gate_blocks * gate_live[:, None, None].astype(jnp.bfloat16)
    w_down = down_blocks * down_live[:, None, None].astype(jnp.bfloat16)
    x_up = jnp.take(x_split, up_major, axis=1)
    x_gate = jnp.take(x_split, gate_major, axis=1)
    up_terms = jnp.einsum("tsi,sij->tsj", x_up, w_up, preferred_element_type=f32)
    gate_terms = jnp.einsum("tsi,sij->tsj", x_gate, w_gate, preferred_element_type=f32)
    up_value = jnp.einsum("tsj,sh->thj", up_terms, up_hidhot, precision=highest)
    gate_value = jnp.einsum("tsj,sh->thj", gate_terms, gate_hidhot, precision=highest)
    sig = 1.0 / (1.0 + jnp.exp(-gate_value))
    act = gate_value * sig
    hidden = (act * up_value).astype(jnp.bfloat16)
    hid_down = jnp.take(hidden, down_minor, axis=1)
    out_terms = jnp.einsum("tsj,sjk->tsk", hid_down, w_down, preferred_element_type=f32)
    partial_out = jnp.einsum("tsk,sc->tck", out_terms, down_colhot, precision=highest).reshape(
        row_total, -1
    )
    out_share = lax.psum_scatter(partial_out, "tensor", scatter_dimension=0, tiled=True)
    dy_split = dy_full.reshape(row_total, width_blocks, block_size)
    dy_down = jnp.take(dy_split, down_major, axis=1)
    dh_terms = jnp.einsum("tsk,sjk->tsj", dy_down, w_down, preferred_element_type=f32)
    d_hidden = jnp.einsum("tsj,sh->thj", dh_terms, down_hidhot, precision=highest)
    d_up = (d_hidden * act).astype(jnp.bfloat16)
    d_gate = (d_hidden * up_value * sig * (1.0 + gate_value * (1.0 - sig))).astype(jnp.bfloat16)
    dup_slots = jnp.take(d_up, up_minor, axis=1)
    dgate_slots = jnp.take(d_gate, gate_minor, axis=1)
    dx_up = jnp.einsum("tsj,sij->tsi", dup_slots, w_up, preferred_element_type=f32)
    dx_gate = jnp.einsum("tsj,sij->tsi", dgate_slots, w_gate, preferred_element_type=f32)
    partial_dx = jnp.einsum("tsi,sr->tri", dx_up, up_rowhot, precision=highest)
    partial_dx = partial_dx + jnp.einsum("tsi,sr->tri", dx_gate, gate_rowhot, precision=highest)
    partial_dx = partial_dx.reshape(row_total, -1)
    dx_share = lax.psum_scatter(partial_dx, "tensor", scatter_dimension=0, tiled=True)
    grad_up = (
        jnp.einsum("tsi,tsj->sij", x_up, dup_slots, preferred_element_type=f32)
        * up_live[:, None, None]
    ).astype(jnp.bfloat16)
    grad_gate = (
        jnp.einsum("tsi,tsj->sij", x_gate, dgate_slots, preferred_element_type=f32)
        * gate_live[:, None, None]
    ).astype(jnp.bfloat16)
    grad_down = (
        jnp.einsum("tsj,tsk->sjk", hid_down, dy_down, preferred_element_type=f32)
        * down_live[:, None, None]
    ).astype(jnp.bfloat16)
    return (
        out_share.astype(jnp.bfloat16),
        dx_share.astype(jnp.bfloat16),
        grad_up,
        grad_gate,
        grad_down,
    )


def solution(mesh):
    placed = (
        P(("groups", "tensor"), None),
        P(("groups", "tensor"), None),
        P("tensor", None, None),
        P("tensor", None, None),
        P("tensor", None, None),
        P("tensor"),
        P("tensor"),
        P("tensor"),
        P(None, "tensor"),
    )
    return jax.shard_map(
        local,
        mesh=mesh,
        in_specs=placed,
        out_specs=(
            P(("groups", "tensor"), None),
            P(("groups", "tensor"), None),
            P(("groups", "tensor"), None, None),
            P(("groups", "tensor"), None, None),
            P(("groups", "tensor"), None, None),
        ),
        check_vma=False,
    )
```

profile of v0, /device:TPU:0, one launch (start us, length us, event | category | flops | bytes accessed | tf_op | source)
XLA Modules:
  0.0 150.8 jit_solution(14236068998945516922)
XLA Ops:
  0.6 0.7 compare_and_fusion.1
  1.3 24.8 %all-gather = bf16[16,2,8192]{2,1,0:T(2,128)(2,1)S(1)} all-gather(bf16[1,2,8192]{2,1,0:T(2,128)(2,1)} %bitcast.118), channel_id=1, replica_groups=mesh['groups'=2,'tensor'=16] {'tensor'}, dimensions={0}, use_global_device_ids=true | all-gather | bytes 557056 | tf_op jit(solution)/shard_map/all_gather | solution.py:32
  26.1 0.4 reshape.71
  26.5 0.0 copy-start.4
  26.5 0.0 copy-start
  26.5 0.3 copy.44
  26.9 0.6 gather_fusion.1
  27.5 0.0 copy-done.4
  27.5 0.6 fusion.74
  28.1 0.6 fusion.73
  28.8 0.0 copy-done
  28.8 0.0 copy-start.5
  28.8 0.5 convolution_bitcast_fusion.1
  29.3 0.6 fusion.13
  29.8 0.0 copy-done.5
  29.9 0.6 gather_fusion
  30.5 0.6 fusion.72
  31.2 0.0 copy-start.6
  31.2 0.0 copy-start.3
  31.2 1.7 %convolution_bitcast_fusion.2 = f32[32,32,128]{2,0,1:T(8,128)S(1)} fusion(bf16[32,128,128]{2,1,0:T(8,128)(2,1)} %param.16, bf16[32]{0:T(256)(128)(2,1)S(1)} %fusion.72, bf16[32,32,128]{2,1,0:T(8,128)(2,1)S(1)} %gather_fusion, pred[32]{0:T(512)(128)(4,1)S(1)} %get-tuple-element.26), kind=kOutput, calls=%fused_computation.12 | convolution fusion | flops 35782656 | bytes 1835104 | tf_op jit(solution)/shard_map/tsi,sij->tsj/dot_general | solution.py:54
  32.9 0.6 fusion.15
  33.5 0.0 copy-done.6
  33.5 0.0 copy-done.3
  33.5 18.9 %all-gather.1 = bf16[16,2,8192]{2,1,0:T(2,128)(2,1)S(1)} all-gather(bf16[1,2,8192]{2,1,0:T(2,128)(2,1)S(1)} %bitcast.119), channel_id=1, replica_groups=mesh['groups'=2,'tensor'=16] {'tensor'}, dimensions={0}, use_global_device_ids=true | all-gather | bytes 557056 | tf_op jit(solution)/shard_map/all_gather | solution.py:33
  52.4 0.4 reshape.73
  52.8 0.3 copy.51
  53.2 0.6 gather_fusion.3
  53.8 0.6 fusion.71
  54.3 1.9 %convolution_bitcast_fusion.5 = f32[32,32,128]{2,0,1:T(8,128)S(1)} fusion(bf16[32,128,128]{2,1,0:T(8,128)(2,1)} %param.17, bf16[32]{0:T(256)(128)(2,1)S(1)} %fusion.71, bf16[32,32,128]{2,1,0:T(8,128)(2,1)S(1)} %gather_fusion.3, pred[32]{0:T(512)(128)(4,1)S(1)} %get-tuple-element.13), kind=kOutput, calls=%fused_computation.15 | convolution fusion | flops 34209792 | bytes 1835104 | tf_op jit(solution)/shard_map/tsk,sjk->tsj/dot_general | solution.py:68
  56.3 0.6 fusion.9
  57.0 0.6 gather_fusion.4
  57.6 0.7 convolution_bitcast_fusion.4
  58.3 0.0 copy-start.1
  58.3 0.9 fusion.7
  59.3 1.3 gather_fusion.5
  60.6 0.0 copy-done.1
  60.6 1.7 %convolution_bitcast_fusion.3 = f32[32,32,128]{2,0,1:T(8,128)S(1)} fusion(bf16[32,128,128]{2,1,0:T(8,128)(2,1)S(1)} %copy-done.1, bf16[32]{0:T(256)(128)(2,1)S(1)} %fusion.72, bf16[32,32,128]{2,1,0:T(8,128)(2,1)} %gather_fusion.5, pred[32]{0:T(512)(128)(4,1)S(1)} %get-tuple-element.9), kind=kOutput, calls=%fused_computation.13 | convolution fusion | flops 34209792 | bytes 1835104 | tf_op jit(solution)/shard_map/tsj,sij->tsi/dot_general | solution.py:75
  62.2 1.0 convolution_add_fusion
  63.2 0.0 copy-start.2
  63.2 0.6 copy.82
  63.9 0.6 gather_fusion.2
  64.5 0.0 copy-done.2
  64.5 0.5 convolution_bitcast_fusion
  65.0 0.9 fusion.11
  65.9 0.6 copy.83
  66.5 0.0 copy-start.7
  66.5 73.7 %all-reduce.4 = (bf16[32,8192]{1,0:T(8,128)(2,1)}, bf16[32,8192]{1,0:T(8,128)(2,1)}) all-reduce(f32[32,8192]{1,0:T(8,128)S(1)} %bitcast.115, f32[32,8192]{1,0:T(8,128)S(1)} %bitcast.114), channel_id=2, replica_groups=mesh['groups'=2,'tensor'=16] {'tensor'}, use_global_device_ids=true, to_apply=%region_0.3.clone | all-reduce | flops 524288 | bytes 3145728
  140.2 0.0 copy-done.7
  140.2 0.6 dynamic-slice
  141.4 1.7 %dynamic-slice_convert_fusion = (bf16[2,8192]{1,0:T(2,128)(2,1)}, bf16[2,8192]{1,0:T(2,128)(2,1)}) fusion(bf16[32,8192]{1,0:T(8,128)(2,1)} %get-tuple-element.8, u32[]{:T(128)S(6)} %multiply.1, bf16[32,8192]{1,0:T(8,128)(2,1)} %get-tuple-element.7), kind=kLoop, calls=%fused_computation.59 | loop fusion | bytes 131076 | tf_op jit(solution)/shard_map/convert_element_type | solution.py:94
  143.1 0.6 compare_convert_fusion.1
  143.8 2.6 %multiply_convert_fusion.1 = bf16[32,128,128]{2,1,0:T(8,128)(2,1)} fusion(f32[32]{0:T(128)S(1)} %compare_convert_fusion.1, bf16[32,32,128]{2,1,0:T(8,128)(2,1)S(1)} %gather_fusion, pred[32]{0:T(512)(128)(4,1)S(1)} %get-tuple-element.26, bf16[32,32,128]{2,1,0:T(8,128)(2,1)} %gather_fusion.5, pred[32]{0:T(512)(128)(4,1)S(1)} %get-tuple-element.9), kind=kOutput, calls=%fused_computation.7 | convolution fusion | flops 34865152 | bytes 1573056 | tf_op jit(solution)/shard_map/tsi,tsj->sij/dot_general | solution.py:85
  146.3 0.6 compare_convert_fusion
  147.0 1.6 %multiply_convert_fusion.2 = bf16[32,128,128]{2,1,0:T(8,128)(2,1)} fusion(f32[32]{0:T(128)S(1)} %compare_convert_fusion, bf16[32,32,128]{2,1,0:T(8,128)(2,1)S(1)} %gather_fusion.1, pred[32]{0:T(512)(128)(4,1)S(1)} %get-tuple-element.31, bf16[32,32,128]{2,1,0:T(8,128)(2,1)S(1)} %gather_fusion.4, pred[32]{0:T(512)(128)(4,1)S(1)} %get-tuple-element.11), kind=kOutput, calls=%fused_computation.8 | convolution fusion | flops 34865152 | bytes 1573056 | tf_op jit(solution)/shard_map/tsi,tsj->sij/dot_general | solution.py:81
  148.6 0.6 compare_convert_fusion.2
  149.2 1.6 %multiply_convert_fusion = bf16[32,128,128]{2,1,0:T(8,128)(2,1)} fusion(f32[32]{0:T(128)S(1)} %compare_convert_fusion.2, bf16[32,32,128]{2,1,0:T(8,128)(2,1)S(1)} %gather_fusion.2, pred[32]{0:T(512)(128)(4,1)S(1)} %get-tuple-element.24, bf16[32,32,128]{2,1,0:T(8,128)(2,1)S(1)} %gather_fusion.3, pred[32]{0:T(512)(128)(4,1)S(1)} %get-tuple-element.13), kind=kOutput, calls=%fused_computation.6 | convolution fusion | flops 34865152 | bytes 1573056 | tf_op jit(solution)/shard_map/tsj,tsk->sjk/dot_general | solution.py:89
  (15 shorter events, 0.1 us)
Async XLA Ops:
  26.5 1.0 copy-start.4
  26.5 2.2 %copy-start = (bf16[32,128,128]{2,1,0:T(8,128)(2,1)S(1)}, bf16[32,128,128]{2,1,0:T(8,128)(2,1)}, u32[]{:S(2)}) copy-start(bf16[32,128,128]{2,1,0:T(8,128)(2,1)} %param.15) | copy-start | bytes 3145732
  28.8 1.1 copy-start.5
  31.2 2.3 %copy-start.6 = (s32[32]{0:T(128)S(1)}, s32[32]{0:T(128)}, u32[]{:S(2)}) copy-start(s32[32]{0:T(128)} %param.20) | copy-start | bytes 388
  31.2 2.4 %copy-start.3 = (bf16[2,8192]{1,0:T(2,128)(2,1)S(1)}, bf16[2,8192]{1,0:T(2,128)(2,1)}, u32[]{:S(2)}) copy-start(bf16[2,8192]{1,0:T(2,128)(2,1)} %param.14) | copy-start | bytes 98308
  58.3 2.3 %copy-start.1 = (bf16[32,128,128]{2,1,0:T(8,128)(2,1)S(1)}, bf16[32,128,128]{2,1,0:T(8,128)(2,1)}, u32[]{:S(2)}) copy-start(bf16[32,128,128]{2,1,0:T(8,128)(2,1)} %param.16) | copy-start | bytes 3145732
  63.2 1.3 copy-start.2
  66.5 73.7 %copy-start.7 = (u32[32]{0:T(128)S(1)}, u32[32]{0:T(128)}, u32[]{:S(2)}) copy-start(u32[32]{0:T(128)} %constant.59) | copy-start | bytes 388
where the time goes:
time: 151 us
  blocking collectives  117 us (77%)
  matrix products  17.4 us (12%)
  local copies, waits for them, and re-layouts  9.91 us (7%)
  other arithmetic  4.48 us (3%)
  between operations  1.65 us (1%)
    unnamed x1, blocking collectives  73.7 us
    all_gather x1, blocking collectives, local(): x_full = lax.all_gather(tokens, 'tensor', axis=0, tiled=True)  24.8 us
    all_gather x1, blocking collectives, local(): dy_full = lax.all_gather(cotangent, 'tensor', axis=0, tiled=True)  18.9 us

commit v1 on v0

--- a/solution.py
+++ b/solution.py
@@ -4,6 +4,28 @@
 from jax.sharding import PartitionSpec as P
 
 HB_DEV = 3
+
+
+def in_order(parts, dim):
+    dims = list(parts.shape[1:])
+    dims[dim] *= parts.shape[0]
+    return jnp.moveaxis(parts, 0, dim).reshape(dims)
+
+
+def collect(x, axis, dim):
+    size = lax.axis_size(axis)
+    pairs = [(i, (i + 1) % size) for i in range(size)]
+    back = [(b, a) for a, b in pairs]
+    lower, upper = ([], [])
+    for step in range(size - 1):
+        if step % 2 == 0:
+            lower.append(lax.ppermute(lower[-1] if lower else x, axis, pairs))
+        else:
+            upper.append(lax.ppermute(upper[-1] if upper else x, axis, back))
+    blocks = jnp.stack([*lower[::-1], x, *upper])
+    shift = lax.axis_index(axis) - len(lower)
+    blocks = blocks[(jnp.arange(size) - shift) % size]
+    return in_order(blocks, dim)
 
 
 def slot_tables(layout, count, major_size):
@@ -29,7 +51,7 @@
 ):
     highest = lax.Precision.HIGHEST
     f32 = jnp.float32
-    x_full = lax.all_gather(tokens, "tensor", axis=0, tiled=True)
+    x_full = collect(tokens, "tensor", 0)
     dy_full = lax.all_gather(cotangent, "tensor", axis=0, tiled=True)
     row_total = x_full.shape[0]
     block_size = up_blocks.shape[1]

time: 151 us -> 181 us (1.20)
  starting transfers between devices: 0 us -> 32.9 us
  blocking collectives: 117 us -> 97.7 us
  waiting for transfers between devices: 0 us -> 10.5 us
  local copies, waits for them, and re-layouts: 9.91 us -> 14.6 us
  other arithmetic: 4.48 us -> 7.86 us
  matrix products: 17.4 us -> 14.9 us
    ppermute x0 -> x15, starting transfers between devices: none -> 32.9 us  [the longest x7 32 us: collect(): upper.append(lax.ppermute(upper[-1] if upper else x, axis, back))]
    all_gather x1 -> x0, blocking collectives: 24.8 us -> none  [local(): x_full = lax.all_gather(tokens, 'tensor', axis=0, tiled=True)]
    ppermute x0 -> x15, waiting for transfers between devices: none -> 10.5 us  [the longest x8 9.28 us: collect(): lower.append(lax.ppermute(lower[-1] if lower else x, axis, pairs))]
    unnamed x1, blocking collectives: 73.7 us -> 76.6 us
    all_gather x1, blocking collectives: 18.9 us -> 21 us  [local(): dy_full = lax.all_gather(cotangent, 'tensor', axis=0, tiled=True)]
  transfers between devices with their start and end apart: 0 -> 15, of which waited for: 0 -> 9; matrix products, arithmetic and copies ran while one was open for 0% -> 7% of each run, Pallas kernels for 0% -> 0%
where the time goes in v1:
time: 181 us; the launch traced here: 180 us
  blocking collectives  97.7 us (54%)
  starting transfers between devices  32.9 us (18%)
  matrix products  14.9 us (8%)
  local copies, waits for them, and re-layouts  14.6 us (8%)
  waiting for transfers between devices  10.5 us (6%)
  other arithmetic  7.86 us (4%)
  between operations  1.94 us (1%)
    unnamed x1, blocking collectives  76.6 us
    ppermute x7, starting transfers between devices, collect(): upper.append(lax.ppermute(upper[-1] if upper else x, axis, back))  32 us
    all_gather x1, blocking collectives, local(): dy_full = lax.all_gather(cotangent, 'tensor', axis=0, tiled=True)  21 us
    ppermute x8, waiting for transfers between devices, collect(): lower.append(lax.ppermute(lower[-1] if lower else x, axis, pairs))  9.28 us
  transfers between devices with their start and end apart: 15, of which 9 were waited for; matrix products, arithmetic and copies ran while one was open for 7% of the time, Pallas kernels for 0%

profile of v1, /device:TPU:0, one launch (start us, length us, event | category | flops | bytes accessed | tf_op | source)
XLA Modules:
  0.0 180.3 jit_solution(3931051904053956462)
XLA Ops:
  0.6 0.5 collective-permute-start
  1.1 5.1 %collective-permute-start.8 = (bf16[2,8192]{1,0:T(2,128)(2,1)}, bf16[2,8192]{1,0:T(2,128)(2,1)S(1)}, u32[]{:S(2)}, u32[]{:S(2)}) collective-permute-start(bf16[2,8192]{1,0:T(2,128)(2,1)} %param.13), channel_id=1, source_target_pairs={{1,0},{2,1},{3,2},{4,3},{5,4},{6,5},{7,6},{8,7},{9,8},{10,9},{11,1... | collective-permute-start | bytes 98312 | tf_op jit(solution)/shard_map/ppermute | solution.py:24
  6.2 1.4 fusion.76
  7.6 0.6 fusion.73
  8.2 21.0 %all-gather = bf16[16,2,8192]{2,1,0:T(2,128)(2,1)S(1)} all-gather(bf16[1,2,8192]{2,1,0:T(2,128)(2,1)} %bitcast.151), channel_id=1, replica_groups=mesh['groups'=2,'tensor'=16] {'tensor'}, dimensions={0}, use_global_device_ids=true | all-gather | bytes 557056 | tf_op jit(solution)/shard_map/all_gather | solution.py:55
  29.2 0.4 reshape.118
  29.6 0.3 copy.51
  30.0 0.5 compare_and_fusion.2
  30.6 0.6 copy-done.11
  31.1 0.6 gather_fusion.4
  31.8 0.7 convolution_bitcast_fusion.5
  32.5 0.6 fusion.9
  33.1 0.6 compare_and_fusion.1
  33.8 0.6 compare_and_fusion
  34.5 0.4 collective-permute-start.1
  34.9 5.7 %collective-permute-done.1 = bf16[2,8192]{1,0:T(2,128)(2,1)S(1)} collective-permute-done((bf16[2,8192]{1,0:T(2,128)(2,1)S(1)}, bf16[2,8192]{1,0:T(2,128)(2,1)S(1)}, u32[]{:S(2)}, u32[]{:S(2)}) %collective-permute-start.1) | collective-permute-done | bytes 32800 | tf_op jit(solution)/shard_map/ppermute | solution.py:22
  40.6 4.5 %collective-permute-start.9 = (bf16[2,8192]{1,0:T(2,128)(2,1)S(1)}, bf16[2,8192]{1,0:T(2,128)(2,1)S(1)}, u32[]{:S(2)}, u32[]{:S(2)}) collective-permute-start(bf16[2,8192]{1,0:T(2,128)(2,1)S(1)} %collective-permute-done.8), channel_id=1, source_target_pairs={{1,0},{2,1},{3,2},{4,3},{5,4},{6,5},{7,6},{8,7},{9,8},{10,9},{11,1... | collective-permute-start | bytes 98312 | tf_op jit(solution)/shard_map/ppermute | solution.py:24
  45.0 1.5 collective-permute-done.2
  46.6 0.6 fusion.75
  47.3 4.5 %collective-permute-start.10 = (bf16[2,8192]{1,0:T(2,128)(2,1)S(1)}, bf16[2,8192]{1,0:T(2,128)(2,1)S(1)}, u32[]{:S(2)}, u32[]{:S(2)}) collective-permute-start(bf16[2,8192]{1,0:T(2,128)(2,1)S(1)} %collective-permute-done.9), channel_id=1, source_target_pairs={{1,0},{2,1},{3,2},{4,3},{5,4},{6,5},{7,6},{8,7},{9,8},{10,9},{11,1... | collective-permute-start | bytes 98312 | tf_op jit(solution)/shard_map/ppermute | solution.py:24
  51.8 1.0 collective-permute-done.3
  52.7 1.2 compare_convert_fusion
  54.0 4.4 %collective-permute-start.11 = (bf16[2,8192]{1,0:T(2,128)(2,1)S(1)}, bf16[2,8192]{1,0:T(2,128)(2,1)S(1)}, u32[]{:S(2)}, u32[]{:S(2)}) collective-permute-start(bf16[2,8192]{1,0:T(2,128)(2,1)S(1)} %collective-permute-done.10), channel_id=1, source_target_pairs={{1,0},{2,1},{3,2},{4,3},{5,4},{6,5},{7,6},{8,7},{9,8},{10,9},{11,1... | collective-permute-start | bytes 98312 | tf_op jit(solution)/shard_map/ppermute | solution.py:24
  58.4 0.4 collective-permute-done.4
  58.8 1.2 fusion.74
  59.9 0.1 collective-permute-done.11
  60.0 4.4 %collective-permute-start.12 = (bf16[2,8192]{1,0:T(2,128)(2,1)S(1)}, bf16[2,8192]{1,0:T(2,128)(2,1)S(1)}, u32[]{:S(2)}, u32[]{:S(2)}) collective-permute-start(bf16[2,8192]{1,0:T(2,128)(2,1)S(1)} %collective-permute-done.11), channel_id=1, source_target_pairs={{1,0},{2,1},{3,2},{4,3},{5,4},{6,5},{7,6},{8,7},{9,8},{10,9},{11,1... | collective-permute-start | bytes 98312 | tf_op jit(solution)/shard_map/ppermute | solution.py:24
  64.4 0.4 collective-permute-done.5
  64.8 1.2 compare_convert_fusion.1
  66.0 0.1 collective-permute-done.12
  66.0 4.4 %collective-permute-start.13 = (bf16[2,8192]{1,0:T(2,128)(2,1)S(1)}, bf16[2,8192]{1,0:T(2,128)(2,1)S(1)}, u32[]{:S(2)}, u32[]{:S(2)}) collective-permute-start(bf16[2,8192]{1,0:T(2,128)(2,1)S(1)} %collective-permute-done.12), channel_id=1, source_target_pairs={{1,0},{2,1},{3,2},{4,3},{5,4},{6,5},{7,6},{8,7},{9,8},{10,9},{11,1... | collective-permute-start | bytes 98312 | tf_op jit(solution)/shard_map/ppermute | solution.py:24
  70.5 0.4 collective-permute-done.6
  70.8 1.2 compare_convert_fusion.2
  72.0 0.6 dynamic-slice
  73.3 4.7 %collective-permute-start.14 = (bf16[2,8192]{1,0:T(2,128)(2,1)S(1)}, bf16[2,8192]{1,0:T(2,128)(2,1)S(1)}, u32[]{:S(2)}, u32[]{:S(2)}) collective-permute-start(bf16[2,8192]{1,0:T(2,128)(2,1)S(1)} %collective-permute-done.13), channel_id=1, source_target_pairs={{1,0},{2,1},{3,2},{4,3},{5,4},{6,5},{7,6},{8,7},{9,8},{10,9},{11,1... | collective-permute-start | bytes 98312 | tf_op jit(solution)/shard_map/ppermute | solution.py:24
  78.5 1.0 collective-permute-done.14
  79.6 1.6 gather_fusion
  81.2 0.4 reshape_reshape.3
  81.6 0.3 copy.44
  82.0 0.6 gather_fusion.2
  82.6 0.2 copy-done.2
  82.8 0.5 convolution_bitcast_fusion.1
  83.3 0.6 fusion.13
  83.9 0.6 gather_fusion.1
  84.5 1.1 convolution_bitcast_fusion.2
  85.7 0.6 fusion.15
  86.3 0.6 gather_fusion.3
  86.9 0.5 convolution_bitcast_fusion
  87.4 0.2 copy-done.12
  87.6 0.9 fusion.11
  88.5 0.6 copy.83
  89.2 0.6 gather_fusion.5
  89.8 0.7 convolution_bitcast_fusion.4
  90.5 0.9 fusion.7
  91.5 0.6 gather_fusion.6
  92.1 1.9 %convolution_bitcast_fusion.3 = f32[32,32,128]{2,0,1:T(8,128)S(1)} fusion(bf16[32,128,128]{2,1,0:T(8,128)(2,1)} %param.16, bf16[32]{0:T(256)(128)(2,1)S(1)} %copy-done.25, bf16[32,32,128]{2,1,0:T(8,128)(2,1)S(1)} %gather_fusion.6, pred[32]{0:T(512)(128)(4,1)S(1)} %copy-done.32), kind=kOutput, calls=%fused_computation.14 | convolution fusion | flops 34209792 | bytes 1835104 | tf_op jit(solution)/shard_map/tsj,sij->tsi/dot_general | solution.py:97
  94.1 0.9 convolution_add_fusion
  95.0 0.6 copy.82
  95.7 76.6 %all-reduce.4 = (bf16[32,8192]{1,0:T(8,128)(2,1)}, bf16[32,8192]{1,0:T(8,128)(2,1)}) all-reduce(f32[32,8192]{1,0:T(8,128)S(1)} %bitcast.147, f32[32,8192]{1,0:T(8,128)S(1)} %bitcast.148), channel_id=2, replica_groups=mesh['groups'=2,'tensor'=16] {'tensor'}, use_global_device_ids=true, to_apply=%region_0.3.clone | all-reduce | flops 524288 | bytes 3145728
  172.3 1.6 dynamic-slice_convert_fusion.1
  173.9 1.6 dynamic-slice_convert_fusion
  175.4 1.6 multiply_convert_fusion.2
  177.1 1.6 multiply_convert_fusion.1
  178.7 1.6 multiply_convert_fusion
  (111 shorter events, 0.9 us)
Async XLA Ops:
  0.6 33.8 %collective-permute-start = (bf16[2,8192]{1,0:T(2,128)(2,1)}, bf16[2,8192]{1,0:T(2,128)(2,1)S(1)}, u32[]{:S(2)}, u32[]{:S(2)}) collective-permute-start(bf16[2,8192]{1,0:T(2,128)(2,1)} %param.13), channel_id=1, source_target_pairs={{0,1},{1,2},{2,3},{3,4},{4,5},{5,6},{6,7},{7,8},{8,9},{9,10},{10,1... | collective-permute-start | bytes 98312 | tf_op jit(solution)/shard_map/ppermute | solution.py:22
  1.1 39.4 %collective-permute-start.8 = (bf16[2,8192]{1,0:T(2,128)(2,1)}, bf16[2,8192]{1,0:T(2,128)(2,1)S(1)}, u32[]{:S(2)}, u32[]{:S(2)}) collective-permute-start(bf16[2,8192]{1,0:T(2,128)(2,1)} %param.13), channel_id=1, source_target_pairs={{1,0},{2,1},{3,2},{4,3},{5,4},{6,5},{7,6},{8,7},{9,8},{10,9},{11,1... | collective-permute-start | bytes 98312 | tf_op jit(solution)/shard_map/ppermute | solution.py:24
  8.2 23.5 %copy-start.21 = (bf16[32]{0:T(256)(128)(2,1)}, bf16[32]{0:T(256)(128)(2,1)S(1)}, u32[]{:S(2)}) copy-start(bf16[32]{0:T(256)(128)(2,1)S(1)} %fusion.73) | copy-start | bytes 196
  29.2 0.8 copy-start.26
  29.6 2.1 %copy-start = (bf16[32,128,128]{2,1,0:T(8,128)(2,1)S(1)}, bf16[32,128,128]{2,1,0:T(8,128)(2,1)}, u32[]{:S(2)}) copy-start(bf16[32,128,128]{2,1,0:T(8,128)(2,1)} %param.17) | copy-start | bytes 3145732
  30.5 0.6 copy-start.11
  30.5 2.0 %copy-start.29 = (pred[32]{0:T(512)(128)(4,1)}, pred[32]{0:T(512)(128)(4,1)S(1)}, u32[]{:S(2)}) copy-start(pred[32]{0:T(512)(128)(4,1)S(1)} %get-tuple-element.13) | copy-start | bytes 100
  31.7 1.4 copy-start.4
  31.8 1.4 copy-start.27
  31.8 2.0 %copy-start.28 = (s32[32]{0:T(128)S(1)}, s32[32]{0:T(128)}, u32[]{:S(2)}) copy-start(s32[32]{0:T(128)} %param.19) | copy-start | bytes 388
  31.8 40.2 %copy-start.33 = (u32[32]{0:T(128)S(1)}, u32[32]{0:T(128)}, u32[]{:S(2)}) copy-start(u32[32]{0:T(128)} %constant.82) | copy-start | bytes 388
  32.5 45.7 %copy-start.6 = (bf16[2,8192]{1,0:T(2,128)(2,1)S(1)}, bf16[2,8192]{1,0:T(2,128)(2,1)}, u32[]{:S(2)}) copy-start(bf16[2,8192]{1,0:T(2,128)(2,1)} %param.13) | copy-start | bytes 98308
  33.7 0.6 copy-start.13
  33.7 47.4 %copy-start.17 = (s32[32]{0:T(128)}, s32[32]{0:T(128)S(1)}, u32[]{:S(2)}) copy-start(s32[32]{0:T(128)S(1)} %get-tuple-element.12) | copy-start | bytes 388
  33.8 48.8 %copy-start.8 = (pred[32]{0:T(512)(128)(4,1)}, pred[32]{0:T(512)(128)(4,1)S(1)}, u32[]{:S(2)}) copy-start(pred[32]{0:T(512)(128)(4,1)S(1)} %get-tuple-element.31) | copy-start | bytes 100
  34.4 46.8 %copy-start.15 = (s32[32]{0:T(128)}, s32[32]{0:T(128)S(1)}, u32[]{:S(2)}) copy-start(s32[32]{0:T(128)S(1)} %get-tuple-element.10) | copy-start | bytes 388
  34.4 46.8 %copy-start.19 = (s32[32]{0:T(128)}, s32[32]{0:T(128)S(1)}, u32[]{:S(2)}) copy-start(s32[32]{0:T(128)S(1)} %get-tuple-element.27) | copy-start | bytes 388
  34.5 6.1 %collective-permute-start.1 = (bf16[2,8192]{1,0:T(2,128)(2,1)S(1)}, bf16[2,8192]{1,0:T(2,128)(2,1)S(1)}, u32[]{:S(2)}, u32[]{:S(2)}) collective-permute-start(bf16[2,8192]{1,0:T(2,128)(2,1)S(1)} %collective-permute-done), channel_id=1, source_target_pairs={{0,1},{1,2},{2,3},{3,4},{4,5},{5,6},{6,7},{7,8},{8,9},{9,10},{10,1... | collective-permute-start | bytes 98312 | tf_op jit(solution)/shard_map/ppermute | solution.py:22
  40.5 6.0 %collective-permute-start.2 = (bf16[2,8192]{1,0:T(2,128)(2,1)S(1)}, bf16[2,8192]{1,0:T(2,128)(2,1)S(1)}, u32[]{:S(2)}, u32[]{:S(2)}) collective-permute-start(bf16[2,8192]{1,0:T(2,128)(2,1)S(1)} %collective-permute-done.1), channel_id=1, source_target_pairs={{0,1},{1,2},{2,3},{3,4},{4,5},{5,6},{6,7},{7,8},{8,9},{9,10},{10,1... | collective-permute-start | bytes 98312 | tf_op jit(solution)/shard_map/ppermute | solution.py:22
  40.6 6.7 %collective-permute-start.9 = (bf16[2,8192]{1,0:T(2,128)(2,1)S(1)}, bf16[2,8192]{1,0:T(2,128)(2,1)S(1)}, u32[]{:S(2)}, u32[]{:S(2)}) collective-permute-start(bf16[2,8192]{1,0:T(2,128)(2,1)S(1)} %collective-permute-done.8), channel_id=1, source_target_pairs={{1,0},{2,1},{3,2},{4,3},{5,4},{6,5},{7,6},{8,7},{9,8},{10,9},{11,1... | collective-permute-start | bytes 98312 | tf_op jit(solution)/shard_map/ppermute | solution.py:24
  46.6 6.1 %collective-permute-start.3 = (bf16[2,8192]{1,0:T(2,128)(2,1)S(1)}, bf16[2,8192]{1,0:T(2,128)(2,1)S(1)}, u32[]{:S(2)}, u32[]{:S(2)}) collective-permute-start(bf16[2,8192]{1,0:T(2,128)(2,1)S(1)} %collective-permute-done.2), channel_id=1, source_target_pairs={{0,1},{1,2},{2,3},{3,4},{4,5},{5,6},{6,7},{7,8},{8,9},{9,10},{10,1... | collective-permute-start | bytes 98312 | tf_op jit(solution)/shard_map/ppermute | solution.py:22
  47.2 35.4 %copy-start.23 = (bf16[32]{0:T(256)(128)(2,1)}, bf16[32]{0:T(256)(128)(2,1)S(1)}, u32[]{:S(2)}) copy-start(bf16[32]{0:T(256)(128)(2,1)S(1)} %fusion.75) | copy-start | bytes 196
  47.3 6.7 %collective-permute-start.10 = (bf16[2,8192]{1,0:T(2,128)(2,1)S(1)}, bf16[2,8192]{1,0:T(2,128)(2,1)S(1)}, u32[]{:S(2)}, u32[]{:S(2)}) collective-permute-start(bf16[2,8192]{1,0:T(2,128)(2,1)S(1)} %collective-permute-done.9), channel_id=1, source_target_pairs={{1,0},{2,1},{3,2},{4,3},{5,4},{6,5},{7,6},{8,7},{9,8},{10,9},{11,1... | collective-permute-start | bytes 98312 | tf_op jit(solution)/shard_map/ppermute | solution.py:24
  52.7 6.0 %collective-permute-start.4 = (bf16[2,8192]{1,0:T(2,128)(2,1)S(1)}, bf16[2,8192]{1,0:T(2,128)(2,1)S(1)}, u32[]{:S(2)}, u32[]{:S(2)}) collective-permute-start(bf16[2,8192]{1,0:T(2,128)(2,1)S(1)} %collective-permute-done.3), channel_id=1, source_target_pairs={{0,1},{1,2},{2,3},{3,4},{4,5},{5,6},{6,7},{7,8},{8,9},{9,10},{10,1... | collective-permute-start | bytes 98312 | tf_op jit(solution)/shard_map/ppermute | solution.py:22
  54.0 6.0 %collective-permute-start.11 = (bf16[2,8192]{1,0:T(2,128)(2,1)S(1)}, bf16[2,8192]{1,0:T(2,128)(2,1)S(1)}, u32[]{:S(2)}, u32[]{:S(2)}) collective-permute-start(bf16[2,8192]{1,0:T(2,128)(2,1)S(1)} %collective-permute-done.10), channel_id=1, source_target_pairs={{1,0},{2,1},{3,2},{4,3},{5,4},{6,5},{7,6},{8,7},{9,8},{10,9},{11,1... | collective-permute-start | bytes 98312 | tf_op jit(solution)/shard_map/ppermute | solution.py:24
  58.8 6.0 %collective-permute-start.5 = (bf16[2,8192]{1,0:T(2,128)(2,1)S(1)}, bf16[2,8192]{1,0:T(2,128)(2,1)S(1)}, u32[]{:S(2)}, u32[]{:S(2)}) collective-permute-start(bf16[2,8192]{1,0:T(2,128)(2,1)S(1)} %collective-permute-done.4), channel_id=1, source_target_pairs={{0,1},{1,2},{2,3},{3,4},{4,5},{5,6},{6,7},{7,8},{8,9},{9,10},{10,1... | collective-permute-start | bytes 98312 | tf_op jit(solution)/shard_map/ppermute | solution.py:22
  60.0 6.0 %collective-permute-start.12 = (bf16[2,8192]{1,0:T(2,128)(2,1)S(1)}, bf16[2,8192]{1,0:T(2,128)(2,1)S(1)}, u32[]{:S(2)}, u32[]{:S(2)}) collective-permute-start(bf16[2,8192]{1,0:T(2,128)(2,1)S(1)} %collective-permute-done.11), channel_id=1, source_target_pairs={{1,0},{2,1},{3,2},{4,3},{5,4},{6,5},{7,6},{8,7},{9,8},{10,9},{11,1... | collective-permute-start | bytes 98312 | tf_op jit(solution)/shard_map/ppermute | solution.py:24
  64.8 6.0 %collective-permute-start.6 = (bf16[2,8192]{1,0:T(2,128)(2,1)S(1)}, bf16[2,8192]{1,0:T(2,128)(2,1)S(1)}, u32[]{:S(2)}, u32[]{:S(2)}) collective-permute-start(bf16[2,8192]{1,0:T(2,128)(2,1)S(1)} %collective-permute-done.5), channel_id=1, source_target_pairs={{0,1},{1,2},{2,3},{3,4},{4,5},{5,6},{6,7},{7,8},{8,9},{9,10},{10,1... | collective-permute-start | bytes 98312 | tf_op jit(solution)/shard_map/ppermute | solution.py:22
  66.0 7.2 %collective-permute-start.13 = (bf16[2,8192]{1,0:T(2,128)(2,1)S(1)}, bf16[2,8192]{1,0:T(2,128)(2,1)S(1)}, u32[]{:S(2)}, u32[]{:S(2)}) collective-permute-start(bf16[2,8192]{1,0:T(2,128)(2,1)S(1)} %collective-permute-done.12), channel_id=1, source_target_pairs={{1,0},{2,1},{3,2},{4,3},{5,4},{6,5},{7,6},{8,7},{9,8},{10,9},{11,1... | collective-permute-start | bytes 98312 | tf_op jit(solution)/shard_map/ppermute | solution.py:24
  70.8 7.1 %collective-permute-start.7 = (bf16[2,8192]{1,0:T(2,128)(2,1)S(1)}, bf16[2,8192]{1,0:T(2,128)(2,1)S(1)}, u32[]{:S(2)}, u32[]{:S(2)}) collective-permute-start(bf16[2,8192]{1,0:T(2,128)(2,1)S(1)} %collective-permute-done.6), channel_id=1, source_target_pairs={{0,1},{1,2},{2,3},{3,4},{4,5},{5,6},{6,7},{7,8},{8,9},{9,10},{10,1... | collective-permute-start | bytes 98312 | tf_op jit(solution)/shard_map/ppermute | solution.py:22
  73.3 6.3 %collective-permute-start.14 = (bf16[2,8192]{1,0:T(2,128)(2,1)S(1)}, bf16[2,8192]{1,0:T(2,128)(2,1)S(1)}, u32[]{:S(2)}, u32[]{:S(2)}) collective-permute-start(bf16[2,8192]{1,0:T(2,128)(2,1)S(1)} %collective-permute-done.13), channel_id=1, source_target_pairs={{1,0},{2,1},{3,2},{4,3},{5,4},{6,5},{7,6},{8,7},{9,8},{10,9},{11,1... | collective-permute-start | bytes 98312 | tf_op jit(solution)/shard_map/ppermute | solution.py:24
  81.6 1.2 copy-start.2
  82.6 0.7 copy-start.18
  82.8 1.7 copy-start.3
  84.5 1.1 copy-start.16
  85.6 1.3 copy-start.1
  85.6 1.3 copy-start.7
  85.7 1.3 copy-start.22
  86.9 0.7 copy-start.12
  88.5 1.3 copy-start.24
  88.5 1.3 copy-start.31
  89.8 0.8 copy-start.14
  90.5 1.6 copy-start.25
  90.5 1.6 copy-start.32
  92.1 2.0 %copy-start.20 = (s32[32]{0:T(128)S(1)}, s32[32]{0:T(128)}, u32[]{:S(2)}) copy-start(s32[32]{0:T(128)} %copy-done.19) | copy-start | bytes 388
  95.6 79.8 %copy-start.9 = (pred[32]{0:T(512)(128)(4,1)S(1)}, pred[32]{0:T(512)(128)(4,1)}, u32[]{:S(2)}) copy-start(pred[32]{0:T(512)(128)(4,1)} %copy-done.8) | copy-start | bytes 100
  95.6 79.8 %copy-start.34 = (f32[32]{0:T(128)S(1)}, f32[32]{0:T(128)}, u32[]{:S(2)}) copy-start(f32[32]{0:T(128)} %compare_convert_fusion) | copy-start | bytes 388
  172.3 4.8 %copy-start.10 = (pred[32]{0:T(512)(128)(4,1)S(1)}, pred[32]{0:T(512)(128)(4,1)}, u32[]{:S(2)}) copy-start(pred[32]{0:T(512)(128)(4,1)} %get-tuple-element.26) | copy-start | bytes 100
  172.3 4.8 %copy-start.35 = (f32[32]{0:T(128)S(1)}, f32[32]{0:T(128)}, u32[]{:S(2)}) copy-start(f32[32]{0:T(128)} %compare_convert_fusion.1) | copy-start | bytes 388
  177.1 1.7 copy-start.5
  177.1 1.7 copy-start.30
  177.1 1.6 copy-start.36
